TPU v7x, 32 devices: a whole 2x2x4 slice. The times are simulated.
32 devices in a mesh: box: 2 (over y), gx: 8 (over z, x), gy: 2 (over core).
Axes of the slice: x: 2, y: 2, z: 4, core: 2. Of those that a mesh axis runs over, the one named last changes fastest.
Arguments:
- positions: float32 [16, 4, 3, 256], P(('box', 'gx'), 'gy'), parts along dimension 0, may hold values from 0 to 18, as said below
- polarizability: float32 [16, 4, 256], P(('box', 'gx'), 'gy'), parts along dimension 0, may hold values from 0.3 to 1.5
- tile_counts: int32 [16, 4, 2], P(('box', 'gx'), 'gy'), parts along dimension 0, may hold values from 80 to 128, as said below
- molecules: int32 [16, 4, 256], P(('box', 'gx'), 'gy'), parts along dimension 0, may hold values from 0 to 170, as said below
- perm_field: float32 [16, 4, 3, 256], P(('box', 'gx'), 'gy'), parts along dimension 0, may hold values from -6 to 6
- dipoles: float32 [16, 4, 3, 256], P(('box', 'gx'), 'gy'), parts along dimension 0, may hold values from -4 to 4
- past_out: float32 [16, 4, 7, 3, 256], P(('box', 'gx'), 'gy'), parts along dimension 0, may hold values from -4 to 4
- past_res: float32 [16, 4, 7, 3, 256], P(('box', 'gx'), 'gy'), parts along dimension 0, may hold values from -15 to 15
Outputs:
- dipoles_next: float32 [16, 4, 3, 256], P(('box', 'gx'), 'gy'), parts along dimension 0
- diis_weights: float32 [16], P('box'), parts along dimension 0
There are 2 independent parts, one for each index of `box`. A program takes and returns all parts, laid end to end along the dimension named above; each array names one. Nothing has to cross between parts.
Inputs may be any that keep to these rules, and one draw needn't show every extreme that they name: x and y in [0, 9); z of an atom in z-tile t lies in [9 t, 9 t + 9); padded slots carry positions too. `tile_counts`: some z-tile is full. `molecules`: a group holds at most three atoms, all of one z-tile of one cell.
All inputs are finite; a program needn't handle non-finite values.
Results may differ from a plain program's by a relative error of at most 0.0003.
Values sent between devices are 32-bit elements; how exact they have to be, the bound alone decides.
A program may use at most 64 MiB of HBM per device.

v0:
```python
import jax
import jax.numpy as jnp
from jax import lax
from jax.sharding import PartitionSpec as P

ITERS = 2


CELL_SIDE = 9.0
CUTOFF_SQ = 81.0
SOFTENING = 0.25
THOLE_DAMP = 0.39
FAR_LIFT = 1000.0
NEIGHBOUR_X = (1.0, 0.0, 1.0, 1.0)
NEIGHBOUR_Y = (0.0, 1.0, 1.0, -1.0)


def from_behind(block, axis, distance):
    devices = range(lax.axis_size(axis))
    route = [((i - distance) % len(devices), i) for i in devices]
    return lax.ppermute(block, axis, route)


def pair_terms(
    target_coords,
    target_polar,
    target_groups,
    target_occupied,
    source_coords,
    source_polar,
    source_groups,
    source_occupied,
):
    displace = source_coords[:, None, :] - target_coords[:, :, None]
    square_dist = jnp.sum(displace * displace, axis=0) + SOFTENING
    distance = jnp.sqrt(square_dist)
    cube_dist = square_dist * distance
    damped = THOLE_DAMP * cube_dist / jnp.sqrt(target_polar[:, None] * source_polar[None, :])
    damping = jnp.exp(-damped)
    tapering = jnp.square(jnp.maximum(1.0 - square_dist / CUTOFF_SQ, 0.0))
    keeper = (target_groups[:, None] != source_groups[None, :]).astype(jnp.float32)
    weight = tapering * keeper * target_occupied[:, None] * source_occupied[None, :]
    isotropic = weight * -jnp.expm1(-damped) / cube_dist
    tensorial = 3.0 * weight * (1.0 - (1.0 + damped) * damping) / (cube_dist * square_dist)
    return (displace, isotropic, tensorial)


def field_targets(displace, isotropic, tensorial, source_dipole):
    projected = jnp.sum(displace * source_dipole[:, None, :], axis=0)
    return jnp.sum(displace * (tensorial * projected)[None], axis=2) - jnp.sum(
        isotropic[None] * source_dipole[:, None, :], axis=2
    )


def field_sources(displace, isotropic, tensorial, target_dipole):
    projected = jnp.sum(displace * target_dipole[:, :, None], axis=0)
    return jnp.sum(displace * (tensorial * projected)[None], axis=1) - jnp.sum(
        isotropic[None] * target_dipole[:, :, None], axis=1
    )


def tiled(values, filler, tile_count):
    shaped = values.reshape(values.shape[:-1] + (tile_count, values.shape[-1] // tile_count))
    widths = [(0, 0)] * (shaped.ndim - 2) + [(1, 1), (0, 0)]
    return jnp.pad(shaped, widths, constant_values=filler)


def padded_coords(coords, tile_count):
    marker = tiled(jnp.zeros_like(coords), 1.0, tile_count)
    lifted = jnp.array([0.0, 0.0, FAR_LIFT], jnp.float32).reshape(3, 1, 1)
    return tiled(coords, 0.0, tile_count) + marker * lifted


def band_sources(padded, tile_at):
    coords, polarity, groups, occupied, dipole = padded

    def flat_vector(member):
        window_part = lax.dynamic_slice_in_dim(member, tile_at, 3, 2)
        return jnp.transpose(window_part, (1, 0, 2, 3)).reshape(3, -1)

    def flat_scalar(member):
        return lax.dynamic_slice_in_dim(member, tile_at, 3, 1).reshape(-1)

    return (
        flat_vector(coords),
        flat_scalar(polarity),
        flat_scalar(groups),
        flat_scalar(occupied),
        flat_vector(dipole),
    )


def target_tile(own_cell, first_slot, tile_width):
    coords, polarity, groups, occupied = own_cell
    return (
        lax.dynamic_slice_in_dim(coords, first_slot, tile_width, 1),
        lax.dynamic_slice_in_dim(polarity, first_slot, tile_width, 0),
        lax.dynamic_slice_in_dim(groups, first_slot, tile_width, 0),
        lax.dynamic_slice_in_dim(occupied, first_slot, tile_width, 0),
    )


def four_static(packed):
    east_cells = from_behind(packed, "gx", -1)
    next_own, next_east = from_behind((packed[0], east_cells[0]), "gy", -1)
    prior_east = from_behind(east_cells[-1], "gy", 1)
    north_cells = jnp.concatenate([packed[1:], next_own[None]], axis=0)
    north_east = jnp.concatenate([east_cells[1:], next_east[None]], axis=0)
    south_east = jnp.concatenate([prior_east[None], east_cells[:-1]], axis=0)
    return jnp.stack([east_cells, north_cells, north_east, south_east], axis=1)


def four_dipole(dipole):
    east_cells = from_behind(dipole, "gx", -1)
    next_own, next_east = from_behind((dipole[0], east_cells[0]), "gy", -1)
    prior_east = from_behind(east_cells[-1], "gy", 1)
    north_cells = jnp.concatenate([dipole[1:], next_own[None]], axis=0)
    north_east = jnp.concatenate([east_cells[1:], next_east[None]], axis=0)
    south_east = jnp.concatenate([prior_east[None], east_cells[:-1]], axis=0)
    return jnp.stack([east_cells, north_cells, north_east, south_east], axis=1)


def half_statics(coords, polarity, groups, occupied, tile_count):
    cell_count = coords.shape[0]
    packed = jnp.concatenate([coords, polarity[:, None], occupied[:, None]], axis=1)
    nearby = four_static(packed)
    lift_x = jnp.array(NEIGHBOUR_X, jnp.float32) * CELL_SIDE
    lift_y = jnp.array(NEIGHBOUR_Y, jnp.float32) * CELL_SIDE
    lifted = jnp.stack([lift_x, lift_y, jnp.zeros_like(lift_x)], axis=1)
    nearby_coords = nearby[:, :, 0:3] + lifted[None, :, :, None]
    nearby_groups = jnp.full((cell_count, 4, coords.shape[-1]), -1, jnp.int32)
    own_padded = (
        padded_coords(coords[:, None], tile_count),
        tiled(polarity[:, None], 1.0, tile_count),
        tiled(groups[:, None], -1, tile_count),
        tiled(occupied[:, None], 0.0, tile_count),
    )
    nearby_padded = (
        padded_coords(nearby_coords, tile_count),
        tiled(nearby[:, :, 3], 1.0, tile_count),
        tiled(nearby_groups, -1, tile_count),
        tiled(nearby[:, :, 4], 0.0, tile_count),
    )
    return (own_padded, nearby_padded)


def half_cell(own_cell, own_band, nearby_band, dipole, tile_count):
    tile_width = dipole.shape[-1] // tile_count

    def one_tile(tile_at, carry):
        own_field, back_field = carry
        first_slot = tile_at * tile_width
        target = target_tile(own_cell, first_slot, tile_width)
        target_dipole = lax.dynamic_slice_in_dim(dipole, first_slot, tile_width, 1)
        source = band_sources(own_band, tile_at)
        displace, isotropic, tensorial = pair_terms(
            target[0], target[1], target[2], target[3], source[0], source[1], source[2], source[3]
        )
        inside = field_targets(displace, isotropic, tensorial, source[4])
        source = band_sources(nearby_band, tile_at)
        displace, isotropic, tensorial = pair_terms(
            target[0], target[1], target[2], target[3], source[0], source[1], source[2], source[3]
        )
        outside = field_targets(displace, isotropic, tensorial, source[4])
        returned = field_sources(displace, isotropic, tensorial, target_dipole)
        returned = jnp.transpose(returned.reshape(3, 4, 3, tile_width), (1, 0, 2, 3))
        own_field = lax.dynamic_update_slice_in_dim(own_field, inside + outside, first_slot, 1)
        window = lax.dynamic_slice_in_dim(back_field, tile_at, 3, 2) + returned
        back_field = lax.dynamic_update_slice_in_dim(back_field, window, tile_at, 2)
        return (own_field, back_field)

    initial = (
        jnp.zeros(dipole.shape, jnp.float32),
        jnp.zeros((4, 3, tile_count + 2, tile_width), jnp.float32),
    )
    own_field, back_field = lax.fori_loop(0, tile_count, one_tile, initial)
    return (own_field, back_field[:, :, 1:-1].reshape(4, 3, -1))


def half_field(own_cells, statics, dipole, tile_count):
    own_padded, nearby_padded = statics
    own_band = own_padded + (tiled(dipole[:, None], 0.0, tile_count),)
    nearby_band = nearby_padded + (tiled(four_dipole(dipole), 0.0, tile_count),)

    def per_cell(members):
        return half_cell(members[0], members[1], members[2], members[3], tile_count)

    own_field, back_field = lax.map(per_cell, (own_cells, own_band, nearby_band, dipole))
    north_part = back_field[:, 1]
    north_east = back_field[:, 2]
    south_east = back_field[:, 3]
    from_below, below_east = from_behind((north_part[-1], north_east[-1]), "gy", 1)
    from_above = from_behind(south_east[0], "gy", -1)
    from_south = jnp.concatenate([from_below[None], north_part[:-1]], axis=0)
    from_south_west = jnp.concatenate([below_east[None], north_east[:-1]], axis=0)
    from_north = jnp.concatenate([south_east[1:], from_above[None]], axis=0)
    eastward = back_field[:, 0] + from_south_west + from_north
    from_west = from_behind(eastward, "gx", 1)
    return own_field + from_south + from_west


def diis_weights(gram_matrix):
    lower = jnp.linalg.cholesky(gram_matrix)
    history = gram_matrix.shape[0]
    forward = []
    for row_at in range(history):
        running = jnp.ones((), gram_matrix.dtype)
        for col_at in range(row_at):
            running = running - lower[row_at, col_at] * forward[col_at]
        forward.append(running / lower[row_at, row_at])
    backward = [None] * history
    for row_at in reversed(range(history)):
        running = forward[row_at]
        for col_at in range(row_at + 1, history):
            running = running - lower[col_at, row_at] * backward[col_at]
        backward[row_at] = running / lower[row_at, row_at]
    solved = jnp.stack(backward)
    return solved / jnp.sum(solved)


def body(
    positions, polarizability, tile_counts, molecules, perm_field, dipoles, past_out, past_res
):
    counts = tile_counts[0]
    cell_count = counts.shape[0]
    tile_count = counts.shape[1]
    coords = positions[0]
    atom_slots = coords.shape[-1]
    tile_width = atom_slots // tile_count
    slot_index = lax.broadcasted_iota(jnp.int32, (cell_count, tile_count, tile_width), 2)
    occupied = (slot_index < counts[:, :, None]).astype(jnp.float32).reshape(cell_count, atom_slots)
    polarity = polarizability[0]
    groups = molecules[0]
    own_cells = (coords, polarity, groups, occupied)
    occupied_vec = occupied[:, None, :]
    scaled = occupied_vec * polarity[:, None, :]
    stored_out = jnp.moveaxis(past_out[0], 1, 0) * occupied_vec
    stored_res = jnp.moveaxis(past_res[0], 1, 0) * occupied_vec
    current = dipoles[0] * occupied_vec
    permanent = perm_field[0]
    statics = half_statics(coords, polarity, groups, occupied, tile_count)
    weights = jnp.zeros((stored_out.shape[0] + 1,), jnp.float32)
    for step_at in range(ITERS):
        induced = half_field(own_cells, statics, current, tile_count)
        jacobi = scaled * (permanent + induced)
        residual = jacobi - current
        outputs_all = jnp.concatenate([stored_out, jacobi[None]], 0)
        residual_all = jnp.concatenate([stored_res, residual[None]], 0)
        flattened = residual_all.reshape(residual_all.shape[0], -1)
        local_gram = jnp.dot(
            flattened,
            flattened.T,
            precision=lax.Precision.HIGHEST,
            preferred_element_type=jnp.float32,
        )
        gram_matrix = lax.psum(local_gram, ("gx", "gy"))
        weights = diis_weights(gram_matrix)
        current = jnp.sum(weights[:, None, None, None] * outputs_all, axis=0)
        stored_out = outputs_all[1:]
        stored_res = residual_all[1:]
    return (current[None], weights)


def solution(mesh):
    placed = (
        P(("box", "gx"), "gy", None, None),
        P(("box", "gx"), "gy", None),
        P(("box", "gx"), "gy", None),
        P(("box", "gx"), "gy", None),
        P(("box", "gx"), "gy", None, None),
        P(("box", "gx"), "gy", None, None),
        P(("box", "gx"), "gy", None, None, None),
        P(("box", "gx"), "gy", None, None, None),
    )
    return jax.shard_map(
        body,
        mesh=mesh,
        in_specs=placed,
        out_specs=(P(("box", "gx"), "gy", None, None), P("box")),
        check_vma=False,
    )
```

profile of v0, /device:TPU:0, one launch (start us, length us, event | category | flops | bytes accessed | tf_op | source)
XLA Modules:
  0.0 246.8 jit_solution(973416661079791287)
XLA Ops:
  2.1 6.0 %collective-permute-start.4 = (f32[2,3,256]{2,1,0:T(4,128)S(1)}, f32[2,3,256]{2,1,0:T(4,128)S(1)}, u32[]{:S(2)}, u32[]{:S(2)}) collective-permute-start(f32[2,3,256]{2,1,0:T(4,128)S(1)} %bitcast_multiply_fusion.2), channel_id=1, source_target_pairs={{2,0},{4,2},{6,4},{8,6},{10,8},{12,10},{14,12},{0,14},{3,1},{5,3},... | collective-permute-start | bytes 18440 | tf_op jit(solution)/shard_map/ppermute | solution.py:21
  20.0 23.1 %while.55 = (s32[]{:T(128)}, f32[2,3,256]{2,1,0:T(4,128)S(1)}, f32[2,4,3,256]{3,1,2,0:T(4,128)S(1)}, f32[2,3,256]{2,1,0:T(4,128)S(1)}, f32[2,256]{1,0:T(2,128)S(...) while((s32[]{:T(128)}, f32[2,3,256]{2,1,0:T(4,128)S(1)}, ...), condition=%wide.region_14.15_spmd, body=%wide.region_0.14_spmd.sunk | while | flops 19906180 | bytes 14344956 | solution.py:188
  20.2 11.3 %while.58 = (s32[]{:T(128)}, f32[3,256]{1,0:T(4,128)S(1)}, f32[4,3,4,128]{3,2,0,1:T(4,128)S(1)}, f32[1,3,4,128]{3,2,1,0:T(4,128)S(1)}, f32[3,256]{1,0:T(4,128)S(...) while((s32[]{:T(128)}, f32[3,256]{1,0:T(4,128)S(1)}, ...), condition=%wide.region_13.13_spmd, body=%wide.region_1.12_spmd.sunk | while | flops 19906180 | bytes 14031151 | solution.py:176
  21.9 1.0 fusion.153
  22.8 1.0 fusion.154
  27.5 1.0 fusion.153
  28.5 1.0 fusion.154
  31.7 11.3 %while.58 = (s32[]{:T(128)}, f32[3,256]{1,0:T(4,128)S(1)}, f32[4,3,4,128]{3,2,0,1:T(4,128)S(1)}, f32[1,3,4,128]{3,2,1,0:T(4,128)S(1)}, f32[3,256]{1,0:T(4,128)S(...) while((s32[]{:T(128)}, f32[3,256]{1,0:T(4,128)S(1)}, ...), condition=%wide.region_13.13_spmd, body=%wide.region_1.12_spmd.sunk | while | flops 19906180 | bytes 14031151 | solution.py:176
  34.4 1.0 fusion.154
  40.0 1.0 fusion.154
  44.7 1.5 collective-permute-start.11
  46.2 4.8 %collective-permute-done.11 = f32[2,3,256]{2,1,0:T(4,128)S(1)} collective-permute-done((f32[2,3,256]{2,1,0:T(4,128)S(1)}, f32[2,3,256]{2,1,0:T(4,128)S(1)}, u32[]{:S(2)}, u32[]{:S(2)}) %collective-permute-start.11) | collective-permute-done | bytes 6176 | tf_op jit(solution)/shard_map/ppermute | solution.py:21
  51.3 29.5 %psum.14 = f32[8,8]{0,1:T(8,128)S(1)} all-reduce(f32[8,8]{0,1:T(8,128)S(1)} %convolution_bitcast_fusion.1), channel_id=1, replica_groups=mesh['box'=2,'gx'=8,'gy'=2] {'gx','gy'}, use_global_device_ids=true, to_apply=%region_15.16 | all-reduce | flops 64 | bytes 512 | tf_op jit(solution)/shard_map/psum | solution.py:256
  130.7 3.5 %collective-permute-done.12 = f32[2,3,256]{2,1,0:T(4,128)S(1)} collective-permute-done((f32[2,3,256]{2,1,0:T(4,128)S(1)}, f32[2,3,256]{2,1,0:T(4,128)S(1)}, u32[]{:S(2)}, u32[]{:S(2)}) %collective-permute-start.12) | collective-permute-done | bytes 6176 | tf_op jit(solution)/shard_map/ppermute | solution.py:21
  135.7 23.1 %while.57 = (s32[]{:T(128)}, f32[2,3,256]{2,1,0:T(4,128)S(1)}, f32[2,4,3,256]{3,1,2,0:T(4,128)S(1)}, f32[2,3,256]{2,1,0:T(4,128)S(1)}, f32[2,256]{1,0:T(2,128)S(...) while((s32[]{:T(128)}, f32[2,3,256]{2,1,0:T(4,128)S(1)}, ...), condition=%wide.region_33.35_spmd, body=%wide.region_19.34_spmd.sunk | while | flops 19906180 | bytes 14344960 | solution.py:188
  135.9 11.3 %while.59 = (s32[]{:T(128)}, f32[3,256]{1,0:T(4,128)S(1)}, f32[4,3,4,128]{3,2,0,1:T(4,128)S(1)}, f32[1,3,4,128]{3,2,1,0:T(4,128)S(1)}, f32[3,256]{1,0:T(4,128)S(...) while((s32[]{:T(128)}, f32[3,256]{1,0:T(4,128)S(1)}, ...), condition=%wide.region_32.33_spmd, body=%wide.region_20.32_spmd.sunk | while | flops 19906180 | bytes 14031151 | solution.py:176
  138.6 1.0 fusion.144
  144.2 1.0 fusion.144
  147.5 11.3 %while.59 = (s32[]{:T(128)}, f32[3,256]{1,0:T(4,128)S(1)}, f32[4,3,4,128]{3,2,0,1:T(4,128)S(1)}, f32[1,3,4,128]{3,2,1,0:T(4,128)S(1)}, f32[3,256]{1,0:T(4,128)S(...) while((s32[]{:T(128)}, f32[3,256]{1,0:T(4,128)S(1)}, ...), condition=%wide.region_32.33_spmd, body=%wide.region_20.32_spmd.sunk | while | flops 19906180 | bytes 14031151 | solution.py:176
  149.2 1.0 fusion.143
  150.2 1.0 fusion.144
  155.8 1.0 fusion.144
  160.7 6.1 %collective-permute-done.19 = f32[2,3,256]{2,1,0:T(4,128)S(1)} collective-permute-done((f32[2,3,256]{2,1,0:T(4,128)S(1)}, f32[2,3,256]{2,1,0:T(4,128)S(1)}, u32[]{:S(2)}, u32[]{:S(2)}) %collective-permute-start.19) | collective-permute-done | bytes 6176 | tf_op jit(solution)/shard_map/ppermute | solution.py:21
  167.1 29.5 %psum.15 = f32[8,8]{0,1:T(8,128)S(1)} all-reduce(f32[8,8]{0,1:T(8,128)S(1)} %convolution_bitcast_fusion), channel_id=1, replica_groups=mesh['box'=2,'gx'=8,'gy'=2] {'gx','gy'}, use_global_device_ids=true, to_apply=%region_34.36 | all-reduce | flops 64 | bytes 512 | tf_op jit(solution)/shard_map/psum | solution.py:256
  (472 shorter events, 60.3 us)
Async XLA Ops:
  2.1 14.2 %collective-permute-start.4 = (f32[2,3,256]{2,1,0:T(4,128)S(1)}, f32[2,3,256]{2,1,0:T(4,128)S(1)}, u32[]{:S(2)}, u32[]{:S(2)}) collective-permute-start(f32[2,3,256]{2,1,0:T(4,128)S(1)} %bitcast_multiply_fusion.2), channel_id=1, source_target_pairs={{2,0},{4,2},{6,4},{8,6},{10,8},{12,10},{14,12},{0,14},{3,1},{5,3},... | collective-permute-start | bytes 18440 | tf_op jit(solution)/shard_map/ppermute | solution.py:21
  8.2 8.2 %collective-permute-start.5 = (f32[3,256]{1,0:T(4,128)S(1)}, f32[3,256]{1,0:T(4,128)S(1)}, u32[]{:S(2)}, u32[]{:S(2)}) collective-permute-start(f32[3,256]{1,0:T(4,128)S(1)} %get-tuple-element.1237), channel_id=1, source_target_pairs={{1,0},{0,1},{3,2},{2,3},{5,4},{4,5},{7,6},{6,7},{9,8},{8,9},{11,10... | collective-permute-start | bytes 9224 | tf_op jit(solution)/shard_map/ppermute | solution.py:21
  10.3 7.6 %collective-permute-start = (f32[2,5,256]{2,1,0:T(8,128)S(1)}, f32[2,5,256]{2,1,0:T(8,128)S(1)}, u32[]{:S(2)}, u32[]{:S(2)}) collective-permute-start(f32[2,5,256]{2,1,0:T(8,128)S(1)} %pad_maximum_fusion.4), channel_id=1, source_target_pairs={{2,0},{4,2},{6,4},{8,6},{10,8},{12,10},{14,12},{0,14},{3,1},{5,3},... | collective-permute-start | bytes 30728 | tf_op jit(solution)/shard_map/ppermute | solution.py:21
  10.9 6.1 %collective-permute-start.1 = (f32[5,256]{1,0:T(8,128)S(1)}, f32[5,256]{1,0:T(8,128)S(1)}, u32[]{:S(2)}, u32[]{:S(2)}) collective-permute-start(f32[5,256]{1,0:T(8,128)S(1)} %get-tuple-element.1225), channel_id=1, source_target_pairs={{1,0},{0,1},{3,2},{2,3},{5,4},{4,5},{7,6},{6,7},{9,8},{8,9},{11,10... | collective-permute-start | bytes 15368 | tf_op jit(solution)/shard_map/ppermute | solution.py:21
  16.4 1.2 collective-permute-start.7
  16.7 1.2 collective-permute-start.6
  17.9 1.2 collective-permute-start.3
  18.3 1.2 collective-permute-start.2
  19.9 23.8 %copy-start.3 = (f32[1,2,7,3,256]{4,1,3,2,0:T(2,128)S(1)}, f32[1,2,7,3,256]{4,1,3,2,0:T(2,128)}, u32[]{:S(2)}) copy-start(f32[1,2,7,3,256]{4,1,3,2,0:T(2,128)} %param.28) | copy-start | bytes 129028
  19.9 23.8 %copy-start.4 = (f32[1,2,7,3,256]{4,1,3,2,0:T(2,128)S(1)}, f32[1,2,7,3,256]{4,1,3,2,0:T(2,128)}, u32[]{:S(2)}) copy-start(f32[1,2,7,3,256]{4,1,3,2,0:T(2,128)} %param.27) | copy-start | bytes 129028
  19.9 31.1 %copy-start.2 = (f32[1,2,3,256]{3,1,2,0:T(2,128)S(1)}, f32[1,2,3,256]{3,1,2,0:T(2,128)}, u32[]{:S(2)}) copy-start(f32[1,2,3,256]{3,1,2,0:T(2,128)} %param.26) | copy-start | bytes 18436
  20.0 31.1 %copy-start.5 = (f32[1,2,3,256]{3,1,2,0:T(2,128)S(1)}, f32[1,2,3,256]{3,1,2,0:T(2,128)}, u32[]{:S(2)}) copy-start(f32[1,2,3,256]{3,1,2,0:T(2,128)} %param.25) | copy-start | bytes 18436
  43.1 1.2 collective-permute-start.10
  43.5 1.2 collective-permute-start.9
  43.7 2.5 collective-permute-start.8
  44.7 6.4 %collective-permute-start.11 = (f32[2,3,256]{2,1,0:T(4,128)S(1)}, f32[2,3,256]{2,1,0:T(4,128)S(1)}, u32[]{:S(2)}, u32[]{:S(2)}) collective-permute-start(f32[2,3,256]{2,1,0:T(4,128)S(1)} %fusion.77), channel_id=1, source_target_pairs={{14,0},{0,2},{2,4},{4,6},{6,8},{8,10},{10,12},{12,14},{15,1},{1,3}... | collective-permute-start | bytes 18440 | tf_op jit(solution)/shard_map/ppermute | solution.py:21
  130.4 3.9 %collective-permute-start.12 = (f32[2,3,256]{2,1,0:T(4,128)S(1)}, f32[2,3,256]{2,1,0:T(4,128)S(1)}, u32[]{:S(2)}, u32[]{:S(2)}) collective-permute-start(f32[2,3,256]{2,1,0:T(4,128)S(1)} %fusion.59), channel_id=1, source_target_pairs={{2,0},{4,2},{6,4},{8,6},{10,8},{12,10},{14,12},{0,14},{3,1},{5,3},... | collective-permute-start | bytes 18440 | tf_op jit(solution)/shard_map/ppermute | solution.py:21
  130.7 4.2 %collective-permute-start.13 = (f32[3,256]{1,0:T(4,128)S(1)}, f32[3,256]{1,0:T(4,128)S(1)}, u32[]{:S(2)}, u32[]{:S(2)}) collective-permute-start(f32[3,256]{1,0:T(4,128)S(1)} %get-tuple-element.1231), channel_id=1, source_target_pairs={{1,0},{0,1},{3,2},{2,3},{5,4},{4,5},{7,6},{6,7},{9,8},{8,9},{11,10... | collective-permute-start | bytes 9224 | tf_op jit(solution)/shard_map/ppermute | solution.py:21
  134.3 1.2 collective-permute-start.15
  134.3 1.3 collective-permute-start.14
  158.9 1.2 collective-permute-start.18
  159.3 1.2 collective-permute-start.17
  159.5 1.2 collective-permute-start.16
  160.5 6.4 %collective-permute-start.19 = (f32[2,3,256]{2,1,0:T(4,128)S(1)}, f32[2,3,256]{2,1,0:T(4,128)S(1)}, u32[]{:S(2)}, u32[]{:S(2)}) collective-permute-start(f32[2,3,256]{2,1,0:T(4,128)S(1)} %fusion.75), channel_id=1, source_target_pairs={{14,0},{0,2},{2,4},{4,6},{6,8},{8,10},{10,12},{12,14},{15,1},{1,3}... | collective-permute-start | bytes 18440 | tf_op jit(solution)/shard_map/ppermute | solution.py:21
  (5 other events, 77.2 us)
where the time goes:
time: 249 us; the launch traced here: 247 us
  between operations  92.8 us (37%)
  blocking collectives  59 us (24%)
  other arithmetic  47 us (19%)
  waiting for transfers between devices  18.3 us (7%)
  local copies, waits for them, and re-layouts  15.3 us (6%)
  starting transfers between devices  12.4 us (5%)
    psum x2, blocking collectives, body(): gram_matrix = lax.psum(local_gram, ('gx', 'gy'))  59 us
    ppermute x20, waiting for transfers between devices, from_behind(): return lax.ppermute(block, axis, route)  18.3 us
    ppermute x20, starting transfers between devices, from_behind(): return lax.ppermute(block, axis, route)  12.4 us
    div x16, other arithmetic, pair_terms(): isotropic = weight * -jnp.expm1(-damped) / cube_dist  10.8 us
    reduce_sum x8, other arithmetic, field_sources(): projected = jnp.sum(displace * target_dipole[:, :, None], axis=0)  8.01 us
    mul x8, other arithmetic, field_targets(): tensorial * projected  7.77 us
    reduce_sum x8, other arithmetic, field_sources(): jnp.sum(displace * (tensorial * projected)[None], axis=1)  5.08 us
  transfers between devices with their start and end apart: 20, of which 14 were waited for; matrix products, arithmetic and copies ran while one was open for 3% of the time, Pallas kernels for 0%

commit v1 on v0

v1 whole, which is shorter than its diff:
```python
import functools

import jax
import jax.numpy as jnp
from jax import lax
from jax.experimental import pallas as pl
from jax.experimental.pallas import tpu as pltpu
from jax.sharding import PartitionSpec as P

CELL_SIDE = 9.0
CUTOFF_SQ = 81.0
SOFTENING = 0.25
THOLE_DAMP = 0.39
LANES = 128
SUBLANES = 8
ROWS = 32
MESH = pl.DeviceIdType.MESH

BLOCKS = ((0, 0), (0, 1), (1, 0), (1, 1), (-1, 0), (-1, 1))
PHASES = ((0,), (1,), (2, 3), (4, 5))


def block_row(cell, half, cells):
    if half == 0:
        return cell
    return -1 if cell == cells - 1 else cells


def sources(target_cell, blocks, cells, tiles):
    found = []
    for block in blocks:
        x_offset, half = BLOCKS[block]
        for cell in range(cells):
            if half == 1 and cell not in (0, cells - 1):
                continue
            if abs(block_row(cell, half, cells) - target_cell) > 1:
                continue
            for tile in range(tiles):
                found.append((block, cell, tile, block == 0 and cell == target_cell))
    return found


def kernel(
    nx,
    ny,
    cells,
    slots,
    stat_ref,
    out_hist,
    res_hist,
    own_ref,
    next_ref,
    weight_ref,
    stat_halo,
    hist_halo,
    jac_halo,
    src,
    tgt,
    iso,
    ten,
    acc,
    jac_own,
    vec,
    gram_send,
    gram_recv,
    stat_send_sem,
    stat_recv_sem,
    hist_send_sem,
    hist_recv_sem,
    jac_send_sem,
    jac_recv_sem,
    gram_send_sem,
    gram_recv_sem,
):
    tiles = slots // LANES
    width = cells * 3 * slots
    total = nx * ny
    my_x = lax.axis_index("gx")
    my_y = lax.axis_index("gy")
    me = my_x * ny + my_y

    def other(step):
        flat = lax.rem(me + step, total)
        return {"gx": flat // ny, "gy": lax.rem(flat, ny)}

    barrier = pltpu.get_barrier_semaphore()

    def greet(step, carry):
        pl.semaphore_signal(barrier, inc=1, device_id=other(step), device_id_type=MESH)
        return carry

    lax.fori_loop(1, total, greet, 0)
    pl.semaphore_wait(barrier, total - 1)

    def halo_copies(source, landing, send_sem, recv_sem):
        copies = []
        for at, (x_offset, half) in enumerate(BLOCKS[1:]):
            target = {
                "gx": lax.rem(my_x - x_offset + nx, nx),
                "gy": lax.rem(my_y + half, ny),
            }
            copies.append(
                pltpu.make_async_remote_copy(
                    src_ref=source,
                    dst_ref=landing.at[at],
                    send_sem=send_sem.at[at],
                    recv_sem=recv_sem.at[at],
                    device_id=target,
                    device_id_type=MESH,
                )
            )
        return copies

    stat_copies = halo_copies(stat_ref, stat_halo, stat_send_sem, stat_recv_sem)
    hist_copies = halo_copies(out_hist, hist_halo, hist_send_sem, hist_recv_sem)
    for copy in stat_copies:
        copy.start()
    for copy in hist_copies:
        copy.start()

    def prepare(block, stat):
        x_offset, half = BLOCKS[block]
        row = lax.broadcasted_iota(jnp.int32, (SUBLANES, slots), 0)
        for cell in range(cells):
            span = slice(cell * slots, (cell + 1) * slots)
            shift_y = CELL_SIDE * block_row(cell, half, cells)
            lift = jnp.where(row == 0, CELL_SIDE * x_offset, jnp.where(row == 1, shift_y, 0.0))
            src[block, :, span] = stat[:, span] + lift

    prepare(0, stat_ref)
    for cell in range(cells):
        span = slice(cell * slots, (cell + 1) * slots)
        columns = jnp.transpose(stat_ref[:, span])
        for at, (row, scale, shift) in enumerate(
            (
                (0, 1.0, 0.0),
                (1, 1.0, CELL_SIDE * cell),
                (2, 1.0, 0.0),
                (3, -THOLE_DAMP, 0.0),
                (7, 1.0, 0.0),
            )
        ):
            column = columns[:, row : row + 1] * scale + shift
            tgt[at, span, :] = jnp.broadcast_to(column, (slots, LANES))

    sub = lax.broadcasted_iota(jnp.int32, (SUBLANES, LANES), 0)
    lane = lax.broadcasted_iota(jnp.int32, (SUBLANES, LANES), 1)
    chunks = [slice(at * LANES, (at + 1) * LANES) for at in range(width // LANES)]

    def inner(rows, vector):
        parts = [r * v for r, v in zip(rows, vector)]
        while len(parts) > 1:
            parts = [sum(parts[at : at + 2]) for at in range(0, len(parts), 2)]
        return jnp.sum(parts[0], axis=1, keepdims=True)

    hist_rows = [res_hist[:, chunk] for chunk in chunks]
    past_gram = jnp.zeros((SUBLANES, LANES), jnp.float32)
    for k in range(SUBLANES - 1):
        column = inner(hist_rows, [rows[k : k + 1] for rows in hist_rows])
        past_gram = past_gram + jnp.where(lane == k, column, 0.0)

    tile_index = [
        {key[:3]: at for at, key in enumerate(sources(c, range(len(BLOCKS)), cells, tiles))}
        for c in range(cells)
    ]

    def first_field(phase, first):
        for c in range(cells):
            met = sources(c, phase, cells, tiles)

            def group(step, carry, c=c, met=met):
                local = pl.ds(pl.multiple_of(step * ROWS, ROWS), ROWS)
                at_slot = pl.ds(pl.multiple_of(c * slots + step * ROWS, ROWS), ROWS)
                ax, ay, az, an = (tgt[m, at_slot, :] for m in range(4))
                if first:
                    sums = [jnp.zeros((ROWS, LANES), jnp.float32)] * 3
                else:
                    sums = [acc[c, m, local, :] for m in range(3)]
                for block, cell, tile, same in met:
                    span = slice(cell * slots + tile * LANES, cell * slots + (tile + 1) * LANES)
                    bx, by, bz, bn, vx, vy, vz, bm = (
                        src[block, m : m + 1, span] for m in range(8)
                    )
                    dx, dy, dz = bx - ax, by - ay, bz - az
                    s = dx * dx + dy * dy + dz * dz + SOFTENING
                    inv = lax.rsqrt(s)
                    inv2 = inv * inv
                    inv3 = inv2 * inv
                    minus_x = (s * s) * inv * (an * bn)
                    e = jnp.exp(minus_x)
                    t = jnp.maximum(1.0 - s * (1.0 / CUTOFF_SQ), 0.0)
                    w = t * t * inv3
                    if same:
                        w = jnp.where(tgt[4, at_slot, :] != bm, w, 0.0)
                    rest = 1.0 - e
                    iso_v = w * rest
                    ten_v = w * (3.0 * inv2) * (rest + minus_x * e)
                    where = tile_index[c][(block, cell, tile)]
                    iso[c, where, local, :] = iso_v
                    ten[c, where, local, :] = ten_v
                    q = ten_v * (dx * vx + dy * vy + dz * vz)
                    sums = [
                        sums[0] + (dx * q - iso_v * vx),
                        sums[1] + (dy * q - iso_v * vy),
                        sums[2] + (dz * q - iso_v * vz),
                    ]
                for m in range(3):
                    acc[c, m, local, :] = sums[m]
                return carry

            lax.fori_loop(0, slots // ROWS, group, 0)

    def second_field():
        for c in range(cells):
            met = sources(c, range(len(BLOCKS)), cells, tiles)

            def group(step, carry, c=c, met=met):
                local = pl.ds(pl.multiple_of(step * ROWS, ROWS), ROWS)
                at_slot = pl.ds(pl.multiple_of(c * slots + step * ROWS, ROWS), ROWS)
                ax, ay, az = (tgt[m, at_slot, :] for m in range(3))
                sums = [jnp.zeros((ROWS, LANES), jnp.float32)] * 3
                for block, cell, tile, _ in met:
                    first = cell * slots + tile * LANES
                    bx, by, bz = (src[block, m : m + 1, first : first + LANES] for m in range(3))
                    starts = [(cell * 3 + m) * slots + tile * LANES for m in range(3)]
                    vx, vy, vz = (vec[block : block + 1, at : at + LANES] for at in starts)
                    dx, dy, dz = bx - ax, by - ay, bz - az
                    where = tile_index[c][(block, cell, tile)]
                    iso_v = iso[c, where, local, :]
                    q = ten[c, where, local, :] * (dx * vx + dy * vy + dz * vz)
                    sums = [
                        sums[0] + (dx * q - iso_v * vx),
                        sums[1] + (dy * q - iso_v * vy),
                        sums[2] + (dz * q - iso_v * vz),
                    ]
                for m in range(3):
                    acc[c, m, local, :] = sums[m]
                return carry

            lax.fori_loop(0, slots // ROWS, group, 0)

    def jacobi_rows():
        found = []
        for c in range(cells):
            for m in range(3):
                for tile in range(tiles):
                    part = acc[c, m, tile * LANES : (tile + 1) * LANES, :]
                    field = jnp.sum(jnp.transpose(part), axis=0, keepdims=True)
                    chunk = chunks[len(found)]
                    found.append(own_ref[0:1, chunk] * (own_ref[1:2, chunk] + field))
        return found

    def gram_share(turn, mine):
        gram_send[turn] = mine

        def copy_to(step):
            return pltpu.make_async_remote_copy(
                src_ref=gram_send.at[turn],
                dst_ref=gram_recv.at[turn, step - 1],
                send_sem=gram_send_sem.at[turn],
                recv_sem=gram_recv_sem.at[turn],
                device_id=other(step),
                device_id_type=MESH,
            )

        def send(step, carry):
            copy_to(step).start()
            return carry

        lax.fori_loop(1, total, send, 0)

        def finish():
            landed = gram_recv.at[turn]
            pltpu.make_async_copy(landed, landed, gram_recv_sem.at[turn]).wait()
            summed = mine + jnp.sum(gram_recv[turn], axis=0)
            return summed

        def sent():
            left = gram_recv.at[turn]
            pltpu.make_async_copy(left, left, gram_send_sem.at[turn]).wait()

        return finish, sent

    def mirrored(gram, column, k):
        row = jnp.sum(jnp.where(sub == lane, column, 0.0), axis=0, keepdims=True)
        return jnp.where(lane == k, column, jnp.where(sub == k, row, gram))

    def solve(gram):
        held = jnp.where(lane == SUBLANES, 1.0, gram)
        for k in range(SUBLANES):
            column = jnp.broadcast_to(held[:, k : k + 1], held.shape)
            pivot_row = held[k : k + 1, :] / column[k : k + 1, :]
            held = jnp.where(sub == k, pivot_row, held - column * pivot_row)
        y = jnp.broadcast_to(held[:, SUBLANES : SUBLANES + 1], held.shape)
        return y / jnp.sum(y, axis=0, keepdims=True)

    def mixed(hist, weights, chunk):
        return jnp.sum(weights * hist, axis=0, keepdims=True)

    newest = SUBLANES - 1
    for at, phase in enumerate(PHASES):
        for block in phase:
            if block:
                stat_copies[block - 1].wait_recv()
                prepare(block, stat_halo.at[block - 1])
        first_field(phase, at == 0)

    jacobi = jacobi_rows()
    for row, chunk in zip(jacobi, chunks):
        jac_own[0:1, chunk] = row
    jac_copies = halo_copies(jac_own, jac_halo, jac_send_sem, jac_recv_sem)
    residual = []
    for at, chunk in enumerate(chunks):
        cell, rest = divmod(at, 3 * tiles)
        m, tile = divmod(rest, tiles)
        first = cell * slots + tile * LANES
        residual.append(jacobi[at] - stat_ref[4 + m : 5 + m, first : first + LANES])
    res_rows = [jnp.where(sub == newest, r, rows) for r, rows in zip(residual, hist_rows)]
    column = inner(res_rows, residual)
    finish, first_sent = gram_share(0, jnp.where(lane == newest, column, past_gram))
    for copy in jac_copies:
        copy.start()
    gram = finish()
    gram = mirrored(gram, jnp.broadcast_to(gram[:, newest : newest + 1], gram.shape), newest)
    weights = solve(gram)

    current = []
    for at, chunk in enumerate(chunks):
        row = mixed(out_hist[:, chunk], weights, chunk) + weights[newest : newest + 1] * jacobi[at]
        current.append(row)
        vec[0:1, chunk] = row
    for block in range(1, len(BLOCKS)):
        hist_copies[block - 1].wait_recv()
        jac_copies[block - 1].wait_recv()
        for chunk in chunks:
            vec[block : block + 1, chunk] = (
                mixed(hist_halo[block - 1, :, chunk], weights, chunk)
                + weights[newest : newest + 1] * jac_halo[block - 1, 0:1, chunk]
            )
    second_field()

    jacobi_next = jacobi_rows()
    residual = [a - b for a, b in zip(jacobi_next, current)]
    res_rows = [jnp.where(sub == 0, r, rows) for r, rows in zip(residual, res_rows)]
    column = inner(res_rows, residual)
    finish, second_sent = gram_share(1, jnp.broadcast_to(column, (SUBLANES, LANES)))
    gram = mirrored(gram, finish(), 0)
    weights = solve(gram)
    kept = jnp.where(sub == 0, 0.0, weights)
    for at, chunk in enumerate(chunks):
        cell, rest = divmod(at, 3 * tiles)
        m, tile = divmod(rest, tiles)
        next_ref[0, cell, m : m + 1, tile * LANES : (tile + 1) * LANES] = (
            mixed(out_hist[:, chunk], kept, chunk)
            + weights[newest : newest + 1] * jac_own[0:1, chunk]
            + weights[0:1] * jacobi_next[at]
        )
    weight_ref[0:newest, :] = weights[1:]
    weight_ref[newest:, :] = weights[0:1]

    for copy in stat_copies + hist_copies + jac_copies:
        copy.wait_send()
    first_sent()
    second_sent()


def body(nx, ny, positions, polarizability, tile_counts, molecules, perm_field, dipoles, past_out, past_res):
    cells, tile_count = tile_counts.shape[1:]
    slots = positions.shape[-1]
    tile_width = slots // tile_count
    tiles = slots // LANES
    past = past_out.shape[2]
    assert ny == 2 and nx > 2 and cells > 1 and past + 1 == SUBLANES and slots % LANES == 0
    index = lax.broadcasted_iota(jnp.int32, (cells, tile_count, tile_width), 2)
    occupied = (index < tile_counts[0][:, :, None]).astype(jnp.float32).reshape(cells, slots)
    spread = occupied[:, None, :]
    static = jnp.concatenate(
        [
            positions[0],
            lax.rsqrt(polarizability[0])[:, None],
            dipoles[0] * spread,
            molecules[0].astype(jnp.float32)[:, None],
        ],
        axis=1,
    )
    static = jnp.moveaxis(static, 1, 0).reshape(SUBLANES, cells * slots)
    width = cells * 3 * slots

    def history(stored):
        rows = jnp.moveaxis(stored[0] * spread[:, None], 1, 0).reshape(past, width)
        return jnp.pad(rows, ((0, SUBLANES - past), (0, 0)))

    scaled = jnp.broadcast_to((polarizability[0] * occupied)[:, None], (cells, 3, slots))
    own = jnp.stack([scaled.reshape(width), perm_field[0].reshape(width)])

    halo = len(BLOCKS) - 1
    met = len(sources(0, range(len(BLOCKS)), cells, tiles))
    vmem = pl.BlockSpec(memory_space=pltpu.VMEM)
    pairs_kept = cells * slots * met * LANES
    current, weights = pl.pallas_call(
        functools.partial(kernel, nx, ny, cells, slots),
        out_shape=(
            jax.ShapeDtypeStruct((1, cells, 3, slots), jnp.float32),
            jax.ShapeDtypeStruct((SUBLANES, LANES), jnp.float32),
        ),
        in_specs=[vmem] * 4,
        out_specs=(vmem, vmem),
        scratch_shapes=[
            pltpu.VMEM((halo, SUBLANES, cells * slots), jnp.float32),
            pltpu.VMEM((halo, SUBLANES, width), jnp.float32),
            pltpu.VMEM((halo, 1, width), jnp.float32),
            pltpu.VMEM((halo + 1, SUBLANES, cells * slots), jnp.float32),
            pltpu.VMEM((5, cells * slots, LANES), jnp.float32),
            pltpu.VMEM((cells, met, slots, LANES), jnp.float32),
            pltpu.VMEM((cells, met, slots, LANES), jnp.float32),
            pltpu.VMEM((cells, 3, slots, LANES), jnp.float32),
            pltpu.VMEM((1, width), jnp.float32),
            pltpu.VMEM((SUBLANES, width), jnp.float32),
            pltpu.VMEM((2, SUBLANES, LANES), jnp.float32),
            pltpu.VMEM((2, nx * ny - 1, SUBLANES, LANES), jnp.float32),
            pltpu.SemaphoreType.DMA((halo,)),
            pltpu.SemaphoreType.DMA((halo,)),
            pltpu.SemaphoreType.DMA((halo,)),
            pltpu.SemaphoreType.DMA((halo,)),
            pltpu.SemaphoreType.DMA((halo,)),
            pltpu.SemaphoreType.DMA((halo,)),
            pltpu.SemaphoreType.DMA((2,)),
            pltpu.SemaphoreType.DMA((2,)),
        ],
        compiler_params=pltpu.CompilerParams(
            collective_id=0, has_side_effects=True, vmem_limit_bytes=48 * 1024 * 1024
        ),
        cost_estimate=pl.CostEstimate(
            flops=70 * pairs_kept, bytes_accessed=16 * width * SUBLANES, transcendentals=2 * pairs_kept
        ),
    )(static, history(past_out), history(past_res), own)
    return (current, weights[:, 0])


def solution(mesh):
    cell_axes = P(("box", "gx"), "gy")
    return jax.shard_map(
        functools.partial(body, mesh.shape["gx"], mesh.shape["gy"]),
        mesh=mesh,
        in_specs=(cell_axes,) * 8,
        out_specs=(cell_axes, P("box")),
        check_vma=False,
    )
```

time: 249 us -> 38.9 us (0.16)
  between operations: 92.8 us -> 0.75 us
  blocking collectives: 59 us -> 0 us
  other arithmetic: 47 us -> 0.88 us
  Pallas kernels: 0 us -> 32.1 us
  waiting for transfers between devices: 18.3 us -> 0 us
  starting transfers between devices: 12.4 us -> 0 us
  local copies, waits for them, and re-layouts: 15.3 us -> 4.85 us
    psum x2 -> x0, blocking collectives: 59 us -> none  [body(): gram_matrix = lax.psum(local_gram, ('gx', 'gy'))]
    pallas_call x0 -> x1, Pallas kernels: none -> 32.1 us  [body(): pl.pallas_call(functools.partial(kernel, nx, ny, cells, slots), out_shape...]
    reduce_sum x50 -> x0, other arithmetic: 20 us -> none  [the longest x8 8.01 us: field_sources(): projected = jnp.sum(displace * target_dipole[:, :, None], axis=0)]
    ppermute x20 -> x0, waiting for transfers between devices: 18.3 us -> none  [from_behind(): return lax.ppermute(block, axis, route)]
    ppermute x20 -> x0, starting transfers between devices: 12.4 us -> none  [from_behind(): return lax.ppermute(block, axis, route)]
    div x20 -> x0, other arithmetic: 10.8 us -> none  [the longest x16 10.8 us: pair_terms(): isotropic = weight * -jnp.expm1(-damped) / cube_dist]
    mul x20 -> x2, other arithmetic: 9.2 us -> 0.01 us  [the longest x1 0.01 us: body(): polarizability[0] * occupied]
    another operation x12 -> x1, other arithmetic: 2.87 us -> 0.02 us  [body(): own = jnp.stack([scaled.reshape(width), perm_field[0].reshape(width)])]
  transfers between devices with their start and end apart: 20 -> 0, of which waited for: 14 -> 0; matrix products, arithmetic and copies ran while one was open for 3% -> 0% of each run, Pallas kernels for 0% -> 0%
where the time goes in v1:
time: 38.9 us; the launch traced here: 38.5 us
  Pallas kernels  32.1 us (83%)
  local copies, waits for them, and re-layouts  4.85 us (12%)
  other arithmetic  0.88 us (2%)
  between operations  0.75 us (2%)
    pallas_call x1, Pallas kernels, body(): pl.pallas_call(functools.partial(kernel, nx, ny, cells, slots), out_shape...  32.1 us
    unnamed x16, local copies, waits for them, and re-layouts  4.06 us
    transpose x1, other arithmetic, history(): rows = jnp.moveaxis(stored[0] * spread[:, None], 1, 0).reshape(past, width)  0.84 us

profile of v1, /device:TPU:0, one launch (start us, length us, event | category | flops | bytes accessed | tf_op | source)
XLA Modules:
  0.0 38.5 jit_solution(1370785324423338552)
XLA Ops:
  0.6 0.0 copy-start
  0.6 0.7 %copy-done = s32[1,2,2]{2,1,0:T(2,128)S(1)} copy-done((s32[1,2,2]{2,1,0:T(2,128)S(1)}, s32[1,2,2]{2,1,0:T(2,128)}, u32[]{:S(2)}) %copy-start) | copy-done | bytes 40
  1.3 0.1 broadcast_bitcast_fusion
  1.4 0.8 %fusion = (f32[7,2,3,256]{3,1,2,0:T(2,128)S(1)}, f32[7,2,3,256]{3,1,2,0:T(2,128)S(1)}) fusion(f32[1,2,7,3,256]{4,1,3,2,0:T(2,128)} %param.15, f32[2,256]{1,0:T(2,128)S(1)} %fusion.2, f32[1,2,7,3,256]{4,1,3,2,0:T(2,128)} %param.14), kind=kLoop, calls=%fused_computation.1 | loop fusion | flops 21504 | bytes 174080 | tf_op jit(solution)/shard_map/transpose | solution.py:390
  2.4 0.0 copy-start.2
  2.4 0.7 %copy-done.2 = f32[1,2,3,256]{3,1,2,0:T(2,128)S(1)} copy-done((f32[1,2,3,256]{3,1,2,0:T(2,128)S(1)}, f32[1,2,3,256]{3,1,2,0:T(2,128)}, u32[]{:S(2)}) %copy-start.2) | copy-done | bytes 6168
  3.1 0.0 copy-start.5
  3.1 0.7 %copy-done.5 = s32[1,2,256]{2,1,0:T(2,128)S(1)} copy-done((s32[1,2,256]{2,1,0:T(2,128)S(1)}, s32[1,2,256]{2,1,0:T(2,128)}, u32[]{:S(2)}) %copy-start.5) | copy-done | bytes 2072
  3.8 0.0 copy-start.1
  3.8 0.0 copy-start.3
  3.8 0.7 %copy-done.1 = f32[1,2,256]{2,1,0:T(2,128)S(1)} copy-done((f32[1,2,256]{2,1,0:T(2,128)S(1)}, f32[1,2,256]{2,1,0:T(2,128)}, u32[]{:S(2)}) %copy-start.1) | copy-done | bytes 2072
  4.4 0.0 copy-done.3
  4.5 0.0 copy-start.4
  4.5 0.7 %copy-done.4 = f32[1,2,3,256]{3,1,2,0:T(2,128)S(1)} copy-done((f32[1,2,3,256]{3,1,2,0:T(2,128)S(1)}, f32[1,2,3,256]{3,1,2,0:T(2,128)}, u32[]{:S(2)}) %copy-start.4) | copy-done | bytes 6168
  5.2 32.1 %shard_map.95 = (f32[1,2,3,256]{3,2,1,0:T(4,128)S(1)}, f32[8,128]{1,0:T(8,128)S(1)}) custom-call(f32[8,512]{1,0:T(8,128)S(1)} %bitcast.37, f32[8,1536]{1,0:T(8,128)S(1)} %pad.7.out_hist, f32[8,1536]{1,0:T(8,128)S(1)} %pad.8.res_hist, f32[2,1536]{1,0:T(2,128)S(1)} %pad_maximum_fusion.own_ref), custom_call_target="tpu_custom_call" | custom-call | flops 82575360 | bytes 196608 | tf_op jit(solution)/shard_map/pallas_call | solution.py:400
  37.3 0.6 %copy.17 = f32[1,2,3,256]{3,1,2,0:T(2,128)} copy(f32[1,2,3,256]{3,2,1,0:T(4,128)S(1)} %get-tuple-element.8) | data formatting | bytes 12288
  37.9 0.6 %slice_reduce_fusion = f32[8]{0:T(128)} fusion(f32[8,128]{1,0:T(8,128)S(1)} %get-tuple-element.5), kind=kLoop, calls=%fused_computation.7 | loop fusion | bytes 64 | tf_op jit(solution)/shard_map/slice | solution.py:437
  (19 shorter events, 0.2 us)
Async XLA Ops:
  0.6 0.7 %copy-start = (s32[1,2,2]{2,1,0:T(2,128)S(1)}, s32[1,2,2]{2,1,0:T(2,128)}, u32[]{:S(2)}) copy-start(s32[1,2,2]{2,1,0:T(2,128)} %param.10) | copy-start | bytes 52
  2.4 0.7 %copy-start.2 = (f32[1,2,3,256]{3,1,2,0:T(2,128)S(1)}, f32[1,2,3,256]{3,1,2,0:T(2,128)}, u32[]{:S(2)}) copy-start(f32[1,2,3,256]{3,1,2,0:T(2,128)} %param.13) | copy-start | bytes 18436
  3.1 0.7 %copy-start.5 = (s32[1,2,256]{2,1,0:T(2,128)S(1)}, s32[1,2,256]{2,1,0:T(2,128)}, u32[]{:S(2)}) copy-start(s32[1,2,256]{2,1,0:T(2,128)} %param.11) | copy-start | bytes 6148
  3.8 0.7 %copy-start.1 = (f32[1,2,256]{2,1,0:T(2,128)S(1)}, f32[1,2,256]{2,1,0:T(2,128)}, u32[]{:S(2)}) copy-start(f32[1,2,256]{2,1,0:T(2,128)} %param.9) | copy-start | bytes 6148
  3.8 0.7 %copy-start.3 = (f32[1,2,3,256]{3,1,2,0:T(2,128)S(1)}, f32[1,2,3,256]{3,1,2,0:T(2,128)}, u32[]{:S(2)}) copy-start(f32[1,2,3,256]{3,1,2,0:T(2,128)} %param.8) | copy-start | bytes 18436
  4.5 0.7 %copy-start.4 = (f32[1,2,3,256]{3,1,2,0:T(2,128)S(1)}, f32[1,2,3,256]{3,1,2,0:T(2,128)}, u32[]{:S(2)}) copy-start(f32[1,2,3,256]{3,1,2,0:T(2,128)} %param.12) | copy-start | bytes 18436

commit v2 on v1

v2 whole, which is shorter than its diff:
```python
import functools

import jax
import jax.numpy as jnp
from jax import lax
from jax.experimental import pallas as pl
from jax.experimental.pallas import tpu as pltpu
from jax.sharding import PartitionSpec as P

CELL_SIDE = 9.0
CUTOFF_SQ = 81.0
SOFTENING = 0.25
THOLE_DAMP = 0.39
LANES = 128
SUBLANES = 8
ROWS = 32
MESH = pl.DeviceIdType.MESH

BLOCKS = ((0, 0), (0, 1), (1, 0), (1, 1), (-1, 0), (-1, 1))
PHASES = ((0,), (1,), (2, 3), (4, 5))


def block_row(cell, half, cells):
    if half == 0:
        return cell
    return -1 if cell == cells - 1 else cells


def sources(target_cell, blocks, cells, tiles):
    found = []
    for block in blocks:
        x_offset, half = BLOCKS[block]
        for cell in range(cells):
            if half == 1 and cell not in (0, cells - 1):
                continue
            if abs(block_row(cell, half, cells) - target_cell) > 1:
                continue
            for tile in range(tiles):
                found.append((block, cell, tile, block == 0 and cell == target_cell))
    return found


def kernel(
    nx,
    ny,
    cells,
    slots,
    tile_width,
    counts,
    args,
    outs,
    held,
    stat,
    out_hist,
    res_hist,
    scale,
    stat_halo,
    hist_halo,
    jac_halo,
    src,
    tgt,
    pair,
    acc,
    jac_own,
    vec,
    past_send,
    past_recv,
    row_send,
    row_recv,
    in_sem,
    stat_sem,
    hist_sem,
    jac_sem,
    past_sem,
    row_sem,
):
    next_ref, weight_ref = outs
    positions, polarity, molecules, permanent, dipoles, past_out, past_res = held
    tiles = slots // LANES
    width = cells * 3 * slots
    total = nx * ny
    my_x = lax.axis_index("gx")
    my_y = lax.axis_index("gy")
    me = my_x * ny + my_y

    def other(step):
        flat = lax.rem(me + step, total)
        return {"gx": flat // ny, "gy": lax.rem(flat, ny)}

    barrier = pltpu.get_barrier_semaphore()

    def greet(step, carry):
        pl.semaphore_signal(barrier, inc=1, device_id=other(step), device_id_type=MESH)
        return carry

    lax.fori_loop(1, total, greet, 0)
    fetches = [
        pltpu.make_async_copy(arg.at[0], into, in_sem.at[at])
        for at, (arg, into) in enumerate(zip(args, held))
    ]
    for fetch in fetches:
        fetch.start()

    def halo_copies(source, landing, sems):
        copies = []
        for at, (x_offset, half) in enumerate(BLOCKS[1:]):
            target = {
                "gx": lax.rem(my_x - x_offset + nx, nx),
                "gy": lax.rem(my_y + half, ny),
            }
            copies.append(
                pltpu.make_async_remote_copy(
                    src_ref=source,
                    dst_ref=landing.at[at],
                    send_sem=sems.at[0, at],
                    recv_sem=sems.at[1, at],
                    device_id=target,
                    device_id_type=MESH,
                )
            )
        return copies

    index = lax.broadcasted_iota(jnp.int32, (1, slots), 1)
    occupied = []
    for cell in range(cells):
        live = jnp.zeros((1, slots), jnp.float32)
        for tile in range(slots // tile_width):
            first = tile * tile_width
            inside = jnp.logical_and(index >= first, index < first + counts[0, cell, tile])
            live = jnp.where(inside, 1.0, live)
        occupied.append(live)

    for fetch in fetches:
        fetch.wait()
    for cell in range(cells):
        span = slice(cell * slots, (cell + 1) * slots)
        polar = polarity[cell : cell + 1, :]
        for m in range(3):
            stat[m : m + 1, span] = positions[m, cell : cell + 1, :]
            stat[4 + m : 5 + m, span] = dipoles[m, cell : cell + 1, :] * occupied[cell]
        stat[3:4, span] = lax.rsqrt(polar)
        stat[7:8, span] = molecules[cell : cell + 1, :].astype(jnp.float32)
        scale[0:1, span] = polar * occupied[cell]
    pl.semaphore_wait(barrier, total - 1)
    stat_copies = halo_copies(stat, stat_halo, stat_sem)
    for copy in stat_copies:
        copy.start()

    for stored, hist in ((past_res, res_hist), (past_out, out_hist)):
        hist[SUBLANES - 1 :, :] = jnp.zeros((1, width), jnp.float32)
        for cell in range(cells):
            for m in range(3):
                first = (cell * 3 + m) * slots
                for k in range(SUBLANES - 1):
                    row = stored[k, m, cell : cell + 1, :] * occupied[cell]
                    hist[k : k + 1, first : first + slots] = row

    def prepare(block, block_stat):
        x_offset, half = BLOCKS[block]
        row = lax.broadcasted_iota(jnp.int32, (SUBLANES, slots), 0)
        for cell in range(cells):
            span = slice(cell * slots, (cell + 1) * slots)
            shift_y = CELL_SIDE * block_row(cell, half, cells)
            lift = jnp.where(row == 0, CELL_SIDE * x_offset, jnp.where(row == 1, shift_y, 0.0))
            src[block, :, span] = block_stat[:, span] + lift

    prepare(0, stat)
    for cell in range(cells):
        span = slice(cell * slots, (cell + 1) * slots)
        columns = jnp.transpose(stat[:, span])
        for at, (row, factor, shift) in enumerate(
            (
                (0, 1.0, 0.0),
                (1, 1.0, CELL_SIDE * cell),
                (2, 1.0, 0.0),
                (3, -THOLE_DAMP, 0.0),
                (7, 1.0, 0.0),
            )
        ):
            column = columns[:, row : row + 1] * factor + shift
            tgt[at, span, :] = jnp.broadcast_to(column, (slots, LANES))

    sub = lax.broadcasted_iota(jnp.int32, (SUBLANES, LANES), 0)
    lane = lax.broadcasted_iota(jnp.int32, (SUBLANES, LANES), 1)
    chunks = [slice(at * LANES, (at + 1) * LANES) for at in range(width // LANES)]

    def inner(rows, vector):
        parts = [r * v for r, v in zip(rows, vector)]
        while len(parts) > 1:
            parts = [sum(parts[at : at + 2]) for at in range(0, len(parts), 2)]
        return jnp.sum(parts[0], axis=1, keepdims=True)

    hist_rows = [res_hist[:, chunk] for chunk in chunks]
    past_gram = jnp.zeros((SUBLANES, LANES), jnp.float32)
    for k in range(SUBLANES - 1):
        column = inner(hist_rows, [rows[k : k + 1] for rows in hist_rows])
        past_gram = past_gram + jnp.where(lane == k, column, 0.0)

    tile_index = [
        {key[:3]: at for at, key in enumerate(sources(c, range(len(BLOCKS)), cells, tiles))}
        for c in range(cells)
    ]

    def share(mine, sent, landed, sems):
        sent[...] = mine

        def copy_to(step):
            return pltpu.make_async_remote_copy(
                src_ref=sent,
                dst_ref=landed.at[step - 1],
                send_sem=sems.at[0],
                recv_sem=sems.at[1],
                device_id=other(step),
                device_id_type=MESH,
            )

        def send(step, carry):
            copy_to(step).start()
            return carry

        def start():
            lax.fori_loop(1, total, send, 0)

        def finish():
            pltpu.make_async_copy(landed, landed, sems.at[1]).wait()
            return mine + jnp.sum(landed[...], axis=0)

        def sent_all():
            pltpu.make_async_copy(landed, landed, sems.at[0]).wait()

        return start, finish, sent_all

    start_past, finish_past, past_sent = share(past_gram, past_send, past_recv, past_sem)
    hist_copies = halo_copies(out_hist, hist_halo, hist_sem)

    def first_field(phase, first):
        for c in range(cells):
            met = sources(c, phase, cells, tiles)

            def group(step, carry, c=c, met=met):
                local = pl.ds(pl.multiple_of(step * ROWS, ROWS), ROWS)
                at_slot = pl.ds(pl.multiple_of(c * slots + step * ROWS, ROWS), ROWS)
                ax, ay, az, an = (tgt[m, at_slot, :] for m in range(4))
                if first:
                    sums = [jnp.zeros((ROWS, LANES), jnp.float32)] * 3
                else:
                    sums = [acc[c, m, local, :] for m in range(3)]
                for block, cell, tile, same in met:
                    span = slice(cell * slots + tile * LANES, cell * slots + (tile + 1) * LANES)
                    bx, by, bz, bn, vx, vy, vz, bm = (
                        src[block, m : m + 1, span] for m in range(8)
                    )
                    dx, dy, dz = bx - ax, by - ay, bz - az
                    s = dx * dx + dy * dy + dz * dz + SOFTENING
                    inv = lax.rsqrt(s)
                    inv2 = inv * inv
                    inv3 = inv2 * inv
                    minus_x = (s * s) * inv * (an * bn)
                    e = jnp.exp(minus_x)
                    t = jnp.maximum(CUTOFF_SQ - s, 0.0)
                    w = t * t * inv3
                    if same:
                        w = jnp.where(tgt[4, at_slot, :] != bm, w, 0.0)
                    rest = 1.0 - e
                    iso_v = w * rest
                    ten_v = w * inv2 * (rest + minus_x * e)
                    where = tile_index[c][(block, cell, tile)]
                    pair[0, c, where, local, :] = iso_v
                    pair[1, c, where, local, :] = ten_v
                    q = ten_v * (dx * (3.0 * vx) + dy * (3.0 * vy) + dz * (3.0 * vz))
                    sums = [
                        sums[0] + (dx * q - iso_v * vx),
                        sums[1] + (dy * q - iso_v * vy),
                        sums[2] + (dz * q - iso_v * vz),
                    ]
                for m in range(3):
                    acc[c, m, local, :] = sums[m]
                return carry

            lax.fori_loop(0, slots // ROWS, group, 0)

    def form_tensors():
        for c in range(cells):
            met = sources(c, range(len(BLOCKS)), cells, tiles)

            def group(step, carry, c=c, met=met):
                local = pl.ds(pl.multiple_of(step * ROWS, ROWS), ROWS)
                at_slot = pl.ds(pl.multiple_of(c * slots + step * ROWS, ROWS), ROWS)
                ax, ay, az = (tgt[m, at_slot, :] for m in range(3))
                for at, (block, cell, tile, _) in enumerate(met):
                    first = cell * slots + tile * LANES
                    bx, by, bz = (src[block, m : m + 1, first : first + LANES] for m in range(3))
                    dx, dy, dz = bx - ax, by - ay, bz - az
                    iso_v = pair[0, c, at, local, :]
                    ten_v = pair[1, c, at, local, :] * 3.0
                    tx, ty, tz = ten_v * dx, ten_v * dy, ten_v * dz
                    pair[0, c, at, local, :] = tx * dx - iso_v
                    pair[1, c, at, local, :] = tx * dy
                    pair[2, c, at, local, :] = tx * dz
                    pair[3, c, at, local, :] = ty * dy - iso_v
                    pair[4, c, at, local, :] = ty * dz
                    pair[5, c, at, local, :] = tz * dz - iso_v
                return carry

            lax.fori_loop(0, slots // ROWS, group, 0)

    def second_field():
        for c in range(cells):
            met = sources(c, range(len(BLOCKS)), cells, tiles)

            def group(step, carry, c=c, met=met):
                local = pl.ds(pl.multiple_of(step * ROWS, ROWS), ROWS)
                sums = [jnp.zeros((ROWS, LANES), jnp.float32)] * 3
                for at, (block, cell, tile, _) in enumerate(met):
                    starts = [(cell * 3 + m) * slots + tile * LANES for m in range(3)]
                    vx, vy, vz = (vec[block : block + 1, at : at + LANES] for at in starts)
                    xx, xy, xz, yy, yz, zz = (pair[n, c, at, local, :] for n in range(6))
                    sums = [
                        sums[0] + (xx * vx + xy * vy + xz * vz),
                        sums[1] + (xy * vx + yy * vy + yz * vz),
                        sums[2] + (xz * vx + yz * vy + zz * vz),
                    ]
                for m in range(3):
                    acc[c, m, local, :] = sums[m]
                return carry

            lax.fori_loop(0, slots // ROWS, group, 0)

    def jacobi_rows():
        found = []
        for c in range(cells):
            for m in range(3):
                for tile in range(tiles):
                    part = acc[c, m, tile * LANES : (tile + 1) * LANES, :]
                    field = jnp.sum(jnp.transpose(part), axis=0, keepdims=True)
                    span = slice(tile * LANES, (tile + 1) * LANES)
                    field = permanent[m, c : c + 1, span] + field * (1.0 / CUTOFF_SQ**2)
                    first = c * slots + tile * LANES
                    found.append(scale[0:1, first : first + LANES] * field)
        return found

    def as_row(column):
        return jnp.sum(jnp.where(sub == lane, column, 0.0), axis=0, keepdims=True)

    def mirrored(gram, row, k):
        column = jnp.sum(jnp.where(sub == lane, row, 0.0), axis=1, keepdims=True)
        return jnp.where(lane == k, column, jnp.where(sub == k, row, gram))

    def solve(gram):
        held = jnp.where(lane == SUBLANES, 1.0, gram)
        for k in range(SUBLANES):
            column = jnp.broadcast_to(held[:, k : k + 1], held.shape)
            pivot_row = held[k : k + 1, :] / column[k : k + 1, :]
            held = jnp.where(sub == k, pivot_row, held - column * pivot_row)
        y = jnp.broadcast_to(held[:, SUBLANES : SUBLANES + 1], held.shape)
        return y / jnp.sum(y, axis=0, keepdims=True)

    def mixed(hist, weights, chunk):
        return jnp.sum(weights * hist, axis=0, keepdims=True)

    newest = SUBLANES - 1
    for at, phase in enumerate(PHASES):
        for block in phase:
            if block:
                stat_copies[block - 1].wait_recv()
                prepare(block, stat_halo.at[block - 1])
        if at == len(PHASES) - 1:
            start_past()
            for copy in hist_copies:
                copy.start()
        first_field(phase, at == 0)

    jacobi = jacobi_rows()
    for row, chunk in zip(jacobi, chunks):
        jac_own[0:1, chunk] = row
    jac_copies = halo_copies(jac_own, jac_halo, jac_sem)
    residual = []
    for at, chunk in enumerate(chunks):
        cell, rest = divmod(at, 3 * tiles)
        m, tile = divmod(rest, tiles)
        first = cell * slots + tile * LANES
        residual.append(jacobi[at] - stat[4 + m : 5 + m, first : first + LANES])
    res_rows = [jnp.where(sub == newest, r, rows) for r, rows in zip(residual, hist_rows)]
    row = as_row(inner(res_rows, residual))
    start, finish, first_sent = share(row, row_send.at[0], row_recv.at[0], row_sem.at[0])
    for copy in jac_copies:
        copy.start()
    start()
    form_tensors()
    past_gram = finish_past()
    gram = mirrored(past_gram, finish(), newest)
    weights = solve(gram)

    current = []
    for at, chunk in enumerate(chunks):
        row = mixed(out_hist[:, chunk], weights, chunk) + weights[newest : newest + 1] * jacobi[at]
        current.append(row)
        vec[0:1, chunk] = row
    for block in range(1, len(BLOCKS)):
        hist_copies[block - 1].wait_recv()
        jac_copies[block - 1].wait_recv()
        for chunk in chunks:
            vec[block : block + 1, chunk] = (
                mixed(hist_halo[block - 1, :, chunk], weights, chunk)
                + weights[newest : newest + 1] * jac_halo[block - 1, 0:1, chunk]
            )
    second_field()

    jacobi_next = jacobi_rows()
    residual = [a - b for a, b in zip(jacobi_next, current)]
    res_rows = [jnp.where(sub == 0, r, rows) for r, rows in zip(residual, res_rows)]
    row = as_row(inner(res_rows, residual))
    start, finish, second_sent = share(row, row_send.at[1], row_recv.at[1], row_sem.at[1])
    start()
    gram = mirrored(gram, finish(), 0)
    weights = solve(gram)
    kept = jnp.where(sub == 0, 0.0, weights)
    for at, chunk in enumerate(chunks):
        cell, rest = divmod(at, 3 * tiles)
        m, tile = divmod(rest, tiles)
        next_ref[0, m, cell : cell + 1, tile * LANES : (tile + 1) * LANES] = (
            mixed(out_hist[:, chunk], kept, chunk)
            + weights[newest : newest + 1] * jac_own[0:1, chunk]
            + weights[0:1] * jacobi_next[at]
        )
    column = jnp.concatenate([weights[1:], weights[0:1]], axis=0)
    weight_ref[...] = as_row(column)[0, :SUBLANES]

    for copy in stat_copies + hist_copies + jac_copies:
        copy.wait_send()
    past_sent()
    first_sent()
    second_sent()


def wired(arg_count, nx, ny, cells, slots, tile_width, counts, *refs):
    args, rest = refs[:arg_count], refs[arg_count:]
    outs, rest = rest[:2], rest[2:]
    held, rest = rest[:arg_count], rest[arg_count:]
    kernel(nx, ny, cells, slots, tile_width, counts, args, outs, held, *rest)


def body(nx, ny, positions, polarizability, tile_counts, molecules, perm_field, dipoles, past_out, past_res):
    cells, tile_count = tile_counts.shape[1:]
    slots = positions.shape[-1]
    tile_width = slots // tile_count
    tiles = slots // LANES
    past = past_out.shape[2]
    assert ny == 2 and nx > 2 and cells > 1 and past + 1 == SUBLANES and slots % LANES == 0
    width = cells * 3 * slots

    halo = len(BLOCKS) - 1
    met = len(sources(0, range(len(BLOCKS)), cells, tiles))
    vmem = pl.BlockSpec(memory_space=pltpu.VMEM)
    hbm = pl.BlockSpec(memory_space=pltpu.HBM)
    raw = (
        jnp.swapaxes(positions, 1, 2),
        polarizability,
        molecules,
        jnp.swapaxes(perm_field, 1, 2),
        jnp.swapaxes(dipoles, 1, 2),
        jnp.transpose(past_out, (0, 2, 3, 1, 4)),
        jnp.transpose(past_res, (0, 2, 3, 1, 4)),
    )
    pairs_kept = cells * slots * met * LANES
    current, weights = pl.pallas_call(
        functools.partial(wired, len(raw), nx, ny, cells, slots, tile_width),
        out_shape=(
            jax.ShapeDtypeStruct((1, 3, cells, slots), jnp.float32),
            jax.ShapeDtypeStruct((SUBLANES,), jnp.float32),
        ),
        in_specs=[pl.BlockSpec(memory_space=pltpu.SMEM)] + [hbm] * len(raw),
        out_specs=(vmem, vmem),
        scratch_shapes=[pltpu.VMEM(arg.shape[1:], arg.dtype) for arg in raw]
        + [
            pltpu.VMEM((SUBLANES, cells * slots), jnp.float32),
            pltpu.VMEM((SUBLANES, width), jnp.float32),
            pltpu.VMEM((SUBLANES, width), jnp.float32),
            pltpu.VMEM((1, cells * slots), jnp.float32),
            pltpu.VMEM((halo, SUBLANES, cells * slots), jnp.float32),
            pltpu.VMEM((halo, SUBLANES, width), jnp.float32),
            pltpu.VMEM((halo, 1, width), jnp.float32),
            pltpu.VMEM((halo + 1, SUBLANES, cells * slots), jnp.float32),
            pltpu.VMEM((5, cells * slots, LANES), jnp.float32),
            pltpu.VMEM((6, cells, met, slots, LANES), jnp.float32),
            pltpu.VMEM((cells, 3, slots, LANES), jnp.float32),
            pltpu.VMEM((1, width), jnp.float32),
            pltpu.VMEM((SUBLANES, width), jnp.float32),
            pltpu.VMEM((SUBLANES, LANES), jnp.float32),
            pltpu.VMEM((nx * ny - 1, SUBLANES, LANES), jnp.float32),
            pltpu.VMEM((2, 1, LANES), jnp.float32),
            pltpu.VMEM((2, nx * ny - 1, 1, LANES), jnp.float32),
            pltpu.SemaphoreType.DMA((len(raw),)),
            pltpu.SemaphoreType.DMA((2, halo)),
            pltpu.SemaphoreType.DMA((2, halo)),
            pltpu.SemaphoreType.DMA((2, halo)),
            pltpu.SemaphoreType.DMA((2,)),
            pltpu.SemaphoreType.DMA((2, 2)),
        ],
        compiler_params=pltpu.CompilerParams(
            collective_id=0, has_side_effects=True, vmem_limit_bytes=56 * 1024 * 1024
        ),
        cost_estimate=pl.CostEstimate(
            flops=70 * pairs_kept, bytes_accessed=16 * width * SUBLANES, transcendentals=2 * pairs_kept
        ),
    )(tile_counts, *raw)
    return (jnp.swapaxes(current, 1, 2), weights)


def solution(mesh):
    cell_axes = P(("box", "gx"), "gy")
    return jax.shard_map(
        functools.partial(body, mesh.shape["gx"], mesh.shape["gy"]),
        mesh=mesh,
        in_specs=(cell_axes,) * 8,
        out_specs=(cell_axes, P("box")),
        check_vma=False,
    )
```

time: 38.9 us -> 36.4 us (0.936)
  local copies, waits for them, and re-layouts: 4.85 us -> 1.8 us
  Pallas kernels: 32.1 us -> 33.7 us
  other arithmetic: 0.88 us -> 0 us
    unnamed x16 -> x4, local copies, waits for them, and re-layouts: 4.06 us -> 1.8 us
    pallas_call x1, Pallas kernels: 32.1 us -> 33.7 us  [body(): pl.pallas_call(functools.partial(wired, len(raw), nx, ny, cells, slots, t...]
    transpose x1 -> x0, other arithmetic: 0.84 us -> none  [history(): rows = jnp.moveaxis(stored[0] * spread[:, None], 1, 0).reshape(past, width)]
    slice x1 -> x0, local copies, waits for them, and re-layouts: 0.62 us -> none  [body(): return (current, weights[:, 0])]
where the time goes in v2:
time: 36.4 us; the launch traced here: 36.2 us
  Pallas kernels  33.7 us (93%)
  local copies, waits for them, and re-layouts  1.8 us (5%)
  between operations  0.65 us (2%)
    pallas_call x1, Pallas kernels, body(): pl.pallas_call(functools.partial(wired, len(raw), nx, ny, cells, slots, t...  33.7 us
    unnamed x4, local copies, waits for them, and re-layouts  1.8 us

profile of v2, /device:TPU:0, one launch (start us, length us, event | category | flops | bytes accessed | tf_op | source)
XLA Modules:
  0.0 36.2 jit_solution(2028476386803284708)
XLA Ops:
  0.6 33.7 %shard_map.95 = (f32[1,3,2,256]{3,2,1,0:T(2,128)}, f32[8]{0:T(128)}) custom-call(s32[1,2,2]{2,1,0:T(2,128)} %counts.1, f32[1,3,2,256]{3,2,1,0:T(2,128)} %bitcast.9, f32[1,2,256]{2,1,0:T(2,128)} %refs_1_.1, s32[1,2,256]{2,1,0:T(2,128)} %refs_2_.1, f32[1,3,2,256]{3,2,1,0:T(2,128)} %bitcast.10, f32[1,3,2,256]{3,2,1,0:T(2,128)} %bitcast.11, ...), custom_call_target="tpu_custom_call" | custom-call | flops 82575360 | bytes 196608 | tf_op jit(solution)/shard_map/pallas_call | solution.py:466
  34.4 0.0 copy-start
  34.4 1.3 %copy.12 = f32[1,2,3,256]{3,1,2,0:T(2,128)} copy(f32[1,2,3,256]{3,1,2,0:T(2,128)} %bitcast.6) | data formatting | bytes 12288
  35.7 0.0 copy-done
  35.7 0.5 %copy.13 = f32[8]{0:T(128)} copy(f32[8]{0:T(128)S(1)} %copy-done) | data formatting | bytes 64
Async XLA Ops:
  34.4 1.3 %copy-start = (f32[8]{0:T(128)S(1)}, f32[8]{0:T(128)}, u32[]{:S(2)}) copy-start(f32[8]{0:T(128)} %get-tuple-element.9) | copy-start | bytes 100

commit v3 on v2

--- a/solution.py
+++ b/solution.py
@@ -46,7 +46,6 @@
     cells,
     slots,
     tile_width,
-    counts,
     args,
     outs,
     held,
@@ -75,7 +74,7 @@
     row_sem,
 ):
     next_ref, weight_ref = outs
-    positions, polarity, molecules, permanent, dipoles, past_out, past_res = held
+    positions, polarity, molecules, permanent, dipoles, past_out, past_res, counts = held
     tiles = slots // LANES
     width = cells * 3 * slots
     total = nx * ny
@@ -121,17 +120,17 @@
         return copies
 
     index = lax.broadcasted_iota(jnp.int32, (1, slots), 1)
+    for fetch in fetches:
+        fetch.wait()
     occupied = []
     for cell in range(cells):
         live = jnp.zeros((1, slots), jnp.float32)
         for tile in range(slots // tile_width):
             first = tile * tile_width
-            inside = jnp.logical_and(index >= first, index < first + counts[0, cell, tile])
+            inside = jnp.logical_and(index >= first, index < first + counts[cell, tile])
             live = jnp.where(inside, 1.0, live)
         occupied.append(live)
 
-    for fetch in fetches:
-        fetch.wait()
     for cell in range(cells):
         span = slice(cell * slots, (cell + 1) * slots)
         polar = polarity[cell : cell + 1, :]
@@ -279,7 +278,7 @@
 
             lax.fori_loop(0, slots // ROWS, group, 0)
 
-    def form_tensors():
+    def second_field():
         for c in range(cells):
             met = sources(c, range(len(BLOCKS)), cells, tiles)
 
@@ -287,38 +286,20 @@
                 local = pl.ds(pl.multiple_of(step * ROWS, ROWS), ROWS)
                 at_slot = pl.ds(pl.multiple_of(c * slots + step * ROWS, ROWS), ROWS)
                 ax, ay, az = (tgt[m, at_slot, :] for m in range(3))
-                for at, (block, cell, tile, _) in enumerate(met):
+                sums = [jnp.zeros((ROWS, LANES), jnp.float32)] * 3
+                for block, cell, tile, _ in met:
                     first = cell * slots + tile * LANES
                     bx, by, bz = (src[block, m : m + 1, first : first + LANES] for m in range(3))
-                    dx, dy, dz = bx - ax, by - ay, bz - az
-                    iso_v = pair[0, c, at, local, :]
-                    ten_v = pair[1, c, at, local, :] * 3.0
-                    tx, ty, tz = ten_v * dx, ten_v * dy, ten_v * dz
-                    pair[0, c, at, local, :] = tx * dx - iso_v
-                    pair[1, c, at, local, :] = tx * dy
-                    pair[2, c, at, local, :] = tx * dz
-                    pair[3, c, at, local, :] = ty * dy - iso_v
-                    pair[4, c, at, local, :] = ty * dz
-                    pair[5, c, at, local, :] = tz * dz - iso_v
-                return carry
-
-            lax.fori_loop(0, slots // ROWS, group, 0)
-
-    def second_field():
-        for c in range(cells):
-            met = sources(c, range(len(BLOCKS)), cells, tiles)
-
-            def group(step, carry, c=c, met=met):
-                local = pl.ds(pl.multiple_of(step * ROWS, ROWS), ROWS)
-                sums = [jnp.zeros((ROWS, LANES), jnp.float32)] * 3
-                for at, (block, cell, tile, _) in enumerate(met):
                     starts = [(cell * 3 + m) * slots + tile * LANES for m in range(3)]
                     vx, vy, vz = (vec[block : block + 1, at : at + LANES] for at in starts)
-                    xx, xy, xz, yy, yz, zz = (pair[n, c, at, local, :] for n in range(6))
+                    dx, dy, dz = bx - ax, by - ay, bz - az
+                    where = tile_index[c][(block, cell, tile)]
+                    iso_v = pair[0, c, where, local, :]
+                    q = pair[1, c, where, local, :] * (dx * (3.0 * vx) + dy * (3.0 * vy) + dz * (3.0 * vz))
                     sums = [
-                        sums[0] + (xx * vx + xy * vy + xz * vz),
-                        sums[1] + (xy * vx + yy * vy + yz * vz),
-                        sums[2] + (xz * vx + yz * vy + zz * vz),
+                        sums[0] + (dx * q - iso_v * vx),
+                        sums[1] + (dy * q - iso_v * vy),
+                        sums[2] + (dz * q - iso_v * vz),
                     ]
                 for m in range(3):
                     acc[c, m, local, :] = sums[m]
@@ -386,7 +367,6 @@
     for copy in jac_copies:
         copy.start()
     start()
-    form_tensors()
     past_gram = finish_past()
     gram = mirrored(past_gram, finish(), newest)
     weights = solve(gram)
@@ -433,11 +413,13 @@
     second_sent()
 
 
-def wired(arg_count, nx, ny, cells, slots, tile_width, counts, *refs):
+def wired(arg_count, nx, ny, cells, slots, tile_width, counts_arg, *refs):
     args, rest = refs[:arg_count], refs[arg_count:]
     outs, rest = rest[:2], rest[2:]
     held, rest = rest[:arg_count], rest[arg_count:]
-    kernel(nx, ny, cells, slots, tile_width, counts, args, outs, held, *rest)
+    counts, *rest = rest
+    args, inside = (*args, counts_arg), (*held, counts)
+    kernel(nx, ny, cells, slots, tile_width, args, outs, inside, *rest)
 
 
 def body(nx, ny, positions, polarizability, tile_counts, molecules, perm_field, dipoles, past_out, past_res):
@@ -462,6 +444,9 @@
         jnp.transpose(past_out, (0, 2, 3, 1, 4)),
         jnp.transpose(past_res, (0, 2, 3, 1, 4)),
     )
+    tile_counts, *raw = (
+        pltpu.with_memory_space_constraint(arg, pltpu.HBM) for arg in (tile_counts, *raw)
+    )
     pairs_kept = cells * slots * met * LANES
     current, weights = pl.pallas_call(
         functools.partial(wired, len(raw), nx, ny, cells, slots, tile_width),
@@ -469,10 +454,11 @@
             jax.ShapeDtypeStruct((1, 3, cells, slots), jnp.float32),
             jax.ShapeDtypeStruct((SUBLANES,), jnp.float32),
         ),
-        in_specs=[pl.BlockSpec(memory_space=pltpu.SMEM)] + [hbm] * len(raw),
+        in_specs=[hbm] * (1 + len(raw)),
         out_specs=(vmem, vmem),
         scratch_shapes=[pltpu.VMEM(arg.shape[1:], arg.dtype) for arg in raw]
         + [
+            pltpu.SMEM(tile_counts.shape[1:], tile_counts.dtype),
             pltpu.VMEM((SUBLANES, cells * slots), jnp.float32),
             pltpu.VMEM((SUBLANES, width), jnp.float32),
             pltpu.VMEM((SUBLANES, width), jnp.float32),
@@ -482,7 +468,7 @@
             pltpu.VMEM((halo, 1, width), jnp.float32),
             pltpu.VMEM((halo + 1, SUBLANES, cells * slots), jnp.float32),
             pltpu.VMEM((5, cells * slots, LANES), jnp.float32),
-            pltpu.VMEM((6, cells, met, slots, LANES), jnp.float32),
+            pltpu.VMEM((2, cells, met, slots, LANES), jnp.float32),
             pltpu.VMEM((cells, 3, slots, LANES), jnp.float32),
             pltpu.VMEM((1, width), jnp.float32),
             pltpu.VMEM((SUBLANES, width), jnp.float32),
@@ -490,7 +476,7 @@
             pltpu.VMEM((nx * ny - 1, SUBLANES, LANES), jnp.float32),
             pltpu.VMEM((2, 1, LANES), jnp.float32),
             pltpu.VMEM((2, nx * ny - 1, 1, LANES), jnp.float32),
-            pltpu.SemaphoreType.DMA((len(raw),)),
+            pltpu.SemaphoreType.DMA((len(raw) + 1,)),
             pltpu.SemaphoreType.DMA((2, halo)),
             pltpu.SemaphoreType.DMA((2, halo)),
             pltpu.SemaphoreType.DMA((2, halo)),
@@ -498,7 +484,7 @@
             pltpu.SemaphoreType.DMA((2, 2)),
         ],
         compiler_params=pltpu.CompilerParams(
-            collective_id=0, has_side_effects=True, vmem_limit_bytes=56 * 1024 * 1024
+            collective_id=0, has_side_effects=True, vmem_limit_bytes=24 * 1024 * 1024
         ),
         cost_estimate=pl.CostEstimate(
             flops=70 * pairs_kept, bytes_accessed=16 * width * SUBLANES, transcendentals=2 * pairs_kept

time: 36.4 us -> 33.3 us (0.915)
  Pallas kernels: 33.7 us -> 31.3 us
  local copies, waits for them, and re-layouts: 1.8 us -> 1.11 us
    pallas_call x1, Pallas kernels: 33.7 us -> 31.3 us  [body(): pl.pallas_call(functools.partial(wired, len(raw), nx, ny, cells, slots, t...]
    unnamed x4 -> x2, local copies, waits for them, and re-layouts: 1.8 us -> 1.11 us
where the time goes in v3:
time: 33.3 us; the launch traced here: 33.1 us
  Pallas kernels  31.3 us (94%)
  local copies, waits for them, and re-layouts  1.11 us (3%)
  between operations  0.64 us (2%)
    pallas_call x1, Pallas kernels, body(): pl.pallas_call(functools.partial(wired, len(raw), nx, ny, cells, slots, t...  31.3 us
    unnamed x2, local copies, waits for them, and re-layouts  1.11 us

profile of v3, /device:TPU:0, one launch (start us, length us, event | category | flops | bytes accessed | tf_op | source)
XLA Modules:
  0.0 33.1 jit_solution(3177538921005960421)
XLA Ops:
  0.6 31.3 %shard_map.95 = (f32[1,3,2,256]{3,2,1,0:T(2,128)S(1)}, f32[8]{0:T(128)S(1)}) custom-call(s32[1,2,2]{2,1,0:T(2,128)} %counts_arg.1, f32[1,3,2,256]{3,2,1,0:T(2,128)} %bitcast.9, f32[1,2,256]{2,1,0:T(2,128)} %refs_1_.1, s32[1,2,256]{2,1,0:T(2,128)} %refs_2_.1, f32[1,3,2,256]{3,2,1,0:T(2,128)} %bitcast.10, f32[1,3,2,256]{3,2,1,0:T(2,128)} %bitcast.11, ...), custom_call_target="tpu_custom_call" | custom-call | flops 82575360 | bytes 196608 | tf_op jit(solution)/shard_map/pallas_call | solution.py:451
  32.0 0.6 %copy.12 = f32[1,2,3,256]{3,1,2,0:T(2,128)} copy(f32[1,2,3,256]{3,1,2,0:T(2,128)S(1)} %bitcast.6) | data formatting | bytes 12288
  32.6 0.5 %copy.13 = f32[8]{0:T(128)} copy(f32[8]{0:T(128)S(1)} %get-tuple-element.9) | data formatting | bytes 64

commit v4 on v3

--- a/solution.py
+++ b/solution.py
@@ -140,10 +140,6 @@
         stat[3:4, span] = lax.rsqrt(polar)
         stat[7:8, span] = molecules[cell : cell + 1, :].astype(jnp.float32)
         scale[0:1, span] = polar * occupied[cell]
-    pl.semaphore_wait(barrier, total - 1)
-    stat_copies = halo_copies(stat, stat_halo, stat_sem)
-    for copy in stat_copies:
-        copy.start()
 
     for stored, hist in ((past_res, res_hist), (past_out, out_hist)):
         hist[SUBLANES - 1 :, :] = jnp.zeros((1, width), jnp.float32)
@@ -340,6 +336,11 @@
         return jnp.sum(weights * hist, axis=0, keepdims=True)
 
     newest = SUBLANES - 1
+    pl.semaphore_wait(barrier, total - 1)
+    stat_copies = halo_copies(stat, stat_halo, stat_sem)
+    for copy in stat_copies:
+        copy.start()
+
     for at, phase in enumerate(PHASES):
         for block in phase:
             if block:

time: 33.3 us -> 32.6 us (0.979)
  Pallas kernels: 31.3 us -> 30.7 us
    pallas_call x1, Pallas kernels: 31.3 us -> 30.7 us  [body(): pl.pallas_call(functools.partial(wired, len(raw), nx, ny, cells, slots, t...]
where the time goes in v4:
time: 32.6 us; the launch traced here: 32.4 us
  Pallas kernels  30.7 us (94%)
  local copies, waits for them, and re-layouts  1.11 us (3%)
  between operations  0.64 us (2%)
    pallas_call x1, Pallas kernels, body(): pl.pallas_call(functools.partial(wired, len(raw), nx, ny, cells, slots, t...  30.7 us
    unnamed x2, local copies, waits for them, and re-layouts  1.11 us

profile of v4, /device:TPU:0, one launch (start us, length us, event | category | flops | bytes accessed | tf_op | source)
XLA Modules:
  0.0 32.4 jit_solution(6654739651100092968)
XLA Ops:
  0.6 30.7 %shard_map.95 = (f32[1,3,2,256]{3,2,1,0:T(2,128)S(1)}, f32[8]{0:T(128)S(1)}) custom-call(s32[1,2,2]{2,1,0:T(2,128)} %counts_arg.1, f32[1,3,2,256]{3,2,1,0:T(2,128)} %bitcast.9, f32[1,2,256]{2,1,0:T(2,128)} %refs_1_.1, s32[1,2,256]{2,1,0:T(2,128)} %refs_2_.1, f32[1,3,2,256]{3,2,1,0:T(2,128)} %bitcast.10, f32[1,3,2,256]{3,2,1,0:T(2,128)} %bitcast.11, ...), custom_call_target="tpu_custom_call" | custom-call | flops 82575360 | bytes 196608 | tf_op jit(solution)/shard_map/pallas_call | solution.py:452
  31.3 0.6 %copy.12 = f32[1,2,3,256]{3,1,2,0:T(2,128)} copy(f32[1,2,3,256]{3,1,2,0:T(2,128)S(1)} %bitcast.6) | data formatting | bytes 12288
  31.9 0.5 %copy.13 = f32[8]{0:T(128)} copy(f32[8]{0:T(128)S(1)} %get-tuple-element.9) | data formatting | bytes 64
